TPU v7x, 32 devices: a whole 2x2x4 slice. The times are simulated.
32 devices in a mesh: sp: 8 (over y, x, core), tp: 4 (over z).
Axes of the slice: x: 2, y: 2, z: 4, core: 2. Of those that a mesh axis runs over, the one named last changes fastest.
Arguments:
- queries: bfloat16 [4096, 8192], P('sp', 'tp'), may hold values from -200 to 200
- keys: bfloat16 [4096, 1024], P('sp', 'tp'), may hold values from -6 to 6
- values: bfloat16 [4096, 1024], P('sp', 'tp'), may hold values from -6 to 6
- w_out: bfloat16 [8192, 4096], P('tp'), may hold values from -0.0625 to 0.0625
- lengths: int32 [1], replicated, may hold values from 1 to 4096
- stretch_owner: int32 [8], replicated, may hold values from 0 to 7, as said below
- home_replica: int32 [1], replicated, may hold values from 0 to 7, as said below
Outputs:
- mixed: bfloat16 [4096, 4096], P(('sp', 'tp'))
- cache_keys: bfloat16 [32768, 1024], P('sp', 'tp')
- home_cache_values: bfloat16 [32768, 1024], P('sp', 'tp')
Inputs may be any that keep to these rules, and one draw needn't show every extreme that they name: Stretch c of prompt p stands on replica stretch_owner[p * 8 + c]; every replica appears once. `home_replica`: the prompts' home replicas are distinct; prompt 0's home is (stretch_owner[0] + 8 / 2) modulo 8.
All inputs are finite; a program needn't handle non-finite values.
Results may differ from a plain program's by a relative error of at most 0.014.
Values may be sent and summed in bfloat16 or wider, within the bound.
A program may use at most 128 MiB of HBM per device.

v0:
```python
import functools
import math

import jax
import jax.numpy as jnp
from jax import lax
from jax.experimental import pallas as pl
from jax.experimental.pallas import tpu as pltpu
from jax.sharding import PartitionSpec as P

HEAD_DIM = 128
MAX_STRETCHES = 8
ROW_BLOCK = 512
UNROLL = 4
LOG2E = math.log2(math.e)
FAR = -1e30
MESH = pl.DeviceIdType.MESH


def find(table, value):
    index = jnp.int32(0)
    for j in range(table.shape[0]):
        index = index + jnp.where(table[j] == value, j, 0)
    return index


def attend_kernel(
    stretch, heads, owner_ref, length_ref, home_ref, q_ref, k_ref, v_ref, o_ref, kc_ref, vc_ref,
    stage, sems, top_ref, high_ref, acc_ref, vt_ref, score_ref,
):
    me = lax.axis_index("sp")
    mine = find(owner_ref, me)
    prompt = mine // MAX_STRETCHES
    own = mine % MAX_STRETCHES
    length = length_ref[prompt]
    lanes = q_ref.shape[0]
    group, block, turn = pl.program_id(0), pl.program_id(1), pl.program_id(2)
    columns = pl.ds(pl.multiple_of(group * HEAD_DIM, HEAD_DIM), HEAD_DIM)
    copies = [
        pltpu.make_async_copy(stage.at[i], out.at[:, columns], sems.at[i])
        for i, out in enumerate((kc_ref, vc_ref))
    ]

    @pl.when((block == 0) & (turn == 0))
    def _():
        homed = jnp.int32(0)
        kept = jnp.int32(0)
        for p in range(home_ref.shape[0]):
            here = home_ref[p] == me
            homed = jnp.where(here, p, homed)
            kept = jnp.where(here, length_ref[p], kept)

        def fill(j, _):
            start = pl.multiple_of(owner_ref[homed * MAX_STRETCHES + j] * stretch, stretch)
            target = pl.ds(pl.multiple_of(j * stretch, stretch), stretch)
            position = j * stretch + lax.broadcasted_iota(jnp.int32, (stretch, HEAD_DIM), 0)
            for i, source in enumerate((k_ref, v_ref)):
                block = source[pl.ds(start, stretch), :]
                stage[i, target, :] = jnp.where(position < kept, block, jnp.zeros_like(block))
            return 0

        lax.fori_loop(0, MAX_STRETCHES, fill, 0)
        for copy in copies:
            copy.start()

        def turned(j, _):
            rows = pl.ds(pl.multiple_of(j * stretch, stretch), stretch)
            vt_ref[:HEAD_DIM, rows] = v_ref[rows, :].T
            return 0

        lax.fori_loop(0, v_ref.shape[0] // stretch, turned, 0)
        vt_ref[HEAD_DIM:, :] = jnp.ones((16, v_ref.shape[0]), jnp.bfloat16)

    within = block * lanes + lax.broadcasted_iota(jnp.int32, (1, lanes), 1)
    live = own * stretch + block * lanes < length

    @pl.when(live)
    def _():
        scale = HEAD_DIM ** (-0.5) * LOG2E
        piece = stretch // 2

        def first_row(j):
            return pl.multiple_of(owner_ref[prompt * MAX_STRETCHES + j] * stretch, stretch)

        def score(j, u, c):
            rows = pl.ds(first_row(j) + c * piece, piece)
            query = q_ref[:, u * HEAD_DIM : (u + 1) * HEAD_DIM]
            scores = lax.dot_general(
                k_ref[rows, :], query, (((1,), (1,)), ((), ())), preferred_element_type=jnp.float32
            )
            score_ref[u, c * piece : (c + 1) * piece, :] = scores
            return jnp.max(scores, axis=0, keepdims=True)

        def score_all(j, u):
            highest = [score(j, u, c) for c in range(2)]
            high_ref[u] = functools.reduce(jnp.maximum, highest)

        def spread(j, u, masked, ahead):
            top = top_ref[u]
            start = first_row(j)
            if masked:
                def seen(c):
                    place_of = c * piece + lax.broadcasted_iota(jnp.int32, (piece, lanes), 0)
                    part = score_ref[u, c * piece : (c + 1) * piece, :]
                    return jnp.where(place_of <= within, part, FAR)

                high = functools.reduce(
                    jnp.maximum,
                    [jnp.max(seen(c), axis=0, keepdims=True) for c in range(2)],
                )
            else:
                def seen(c):
                    return score_ref[u, c * piece : (c + 1) * piece, :]

                high = high_ref[u]
            new_top = jnp.maximum(top, high * scale)
            rescale = jnp.exp2(top - new_top)
            highest, weights = [], []
            acc = acc_ref[u] * rescale
            for c in range(2):
                if ahead is not None:
                    highest.append(score(ahead[0], ahead[1], c))
                weights.append(jnp.exp2(seen(c) * scale - new_top).astype(jnp.bfloat16))
            acc = acc + jnp.dot(
                vt_ref[:, pl.ds(start, stretch)], jnp.concatenate(weights, axis=0),
                preferred_element_type=jnp.float32,
            )
            acc_ref[u] = acc
            top_ref[u] = new_top
            if ahead is not None:
                high_ref[ahead[1]] = functools.reduce(jnp.maximum, highest)

        top_ref[...] = jnp.full_like(top_ref, FAR)
        acc_ref[...] = jnp.zeros_like(acc_ref)
        score_all(0, 0)

        def body(j, _):
            for u in range(heads):
                spread(j, u, False, (j, u + 1) if u + 1 < heads else (j + 1, 0))
            return 0

        lax.fori_loop(0, own, body, 0)
        for u in range(heads):
            spread(own, u, True, (own, u + 1) if u + 1 < heads else None)
        alive = (own * stretch + within < length).astype(jnp.float32)
        for u in range(heads):
            out = (acc_ref[u, :HEAD_DIM] * (alive / acc_ref[u, HEAD_DIM : HEAD_DIM + 1])).T
            o_ref[:, u * HEAD_DIM : (u + 1) * HEAD_DIM] = out.astype(jnp.bfloat16)

    @pl.when(jnp.logical_not(live))
    def _():
        o_ref[...] = jnp.zeros_like(o_ref)

    @pl.when((block == pl.num_programs(1) - 1) & (turn == pl.num_programs(2) - 1))
    def _():
        for copy in copies:
            copy.wait()


def attend(stretch, tables, queries, keys, values):
    width = queries.shape[1]
    kv_width = keys.shape[1]
    local_kv = kv_width // HEAD_DIM
    group_size = width // kv_width
    heads = math.gcd(UNROLL, group_size)
    turns = group_size // heads
    lanes = math.gcd(ROW_BLOCK, stretch)
    span = MAX_STRETCHES * stretch
    cache = jax.ShapeDtypeStruct((span, kv_width), jnp.bfloat16)
    query_spec = pl.BlockSpec((lanes, heads * HEAD_DIM), lambda g, r, u, *_: (r, g * turns + u))
    kv_spec = pl.BlockSpec((keys.shape[0], HEAD_DIM), lambda g, r, u, *_: (0, g))
    return pl.pallas_call(
        functools.partial(attend_kernel, stretch, heads),
        out_shape=[jax.ShapeDtypeStruct((stretch, width), jnp.bfloat16), cache, cache],
        grid_spec=pltpu.PrefetchScalarGridSpec(
            num_scalar_prefetch=3,
            grid=(local_kv, stretch // lanes, turns),
            in_specs=[query_spec, kv_spec, kv_spec],
            out_specs=[query_spec] + [pl.BlockSpec(memory_space=pl.ANY)] * 2,
            scratch_shapes=[
                pltpu.VMEM((2, span, HEAD_DIM), jnp.bfloat16),
                pltpu.SemaphoreType.DMA((2,)),
                pltpu.VMEM((heads, 1, lanes), jnp.float32),
                pltpu.VMEM((heads, 1, lanes), jnp.float32),
                pltpu.VMEM((heads, HEAD_DIM + 16, lanes), jnp.float32),
                pltpu.VMEM((HEAD_DIM + 16, values.shape[0]), jnp.bfloat16),
                pltpu.VMEM((heads, stretch, lanes), jnp.float32),
            ],
        ),
        compiler_params=pltpu.CompilerParams(
            dimension_semantics=("arbitrary",) * 3, vmem_limit_bytes=48 * 2**20
        ),
        name="attend",
    )(*tables, queries, keys, values)


def gather(keys, values):
    return (
        lax.all_gather(keys, "sp", axis=0, tiled=True),
        lax.all_gather(values, "sp", axis=0, tiled=True),
    )


def project(attended, w_out):
    partial = jnp.dot(attended, w_out, preferred_element_type=jnp.float32)
    return lax.psum_scatter(
        partial.astype(jnp.bfloat16), "tp", scatter_dimension=0, tiled=True
    )


CHUNKS = 4
UNITS = 4
PASSES = 2
SLICE = 512


def layer_kernel(
    owner_ref, length_ref, home_ref, q_ref, k_ref, v_ref, w_hbm, o_ref, kc_ref, vc_ref,
    all_k, all_v, w_ref, vt_ref, qs_ref, top_ref, acc_ref, high_ref, score_ref, att_ref, stage,
    own_ref, mid_ref, out_far, out_near, out_sum, in_far, in_near, in_sum,
    w_sem, place_sem, cache_sem, send_sem, recv_sem, sum_send, sum_recv,
):
    me = lax.axis_index("sp")
    z = lax.axis_index("tp")
    n = 4
    stretch = k_ref.shape[0]
    kv_width = k_ref.shape[1]
    rows = q_ref.shape[2]
    lanes = score_ref.shape[2]
    per_unit = lanes // (n * rows)
    piece = stretch // 2
    steps = CHUNKS * PASSES
    width = o_ref.shape[1] // PASSES
    y, x, core = me // 4, me // 2 % 2, me % 2

    def flip(bit, by):
        return bit + by - 2 * bit * by

    def source(m):
        return flip(y, m // 4 % 2) * 4 + flip(x, m // 2 % 2) * 2 + flip(core, m % 2)

    partner, beside, above, across = source(1), source(2), source(4), source(6)
    relay_from = core * beside + (1 - core) * above
    relay_to = core * above + (1 - core) * beside

    barrier = pltpu.get_barrier_semaphore()
    for other in (beside, above, partner):
        pl.semaphore_signal(barrier, inc=1, device_id={"sp": other}, device_id_type=MESH)
    for other in ((z + 1) % n, (z + n - 1) % n):
        pl.semaphore_signal(barrier, inc=1, device_id={"tp": other}, device_id_type=MESH)
    pl.semaphore_wait(barrier, 5)

    sources, outs = (k_ref, v_ref), (all_k, all_v)

    def send(i, lane, source, owner, target):
        return pltpu.make_async_remote_copy(
            src_ref=source,
            dst_ref=outs[i].at[owner],
            send_sem=send_sem.at[lane, i],
            recv_sem=recv_sem.at[lane, i],
            device_id={"sp": target},
            device_id_type=MESH,
        )

    sent, places = [], []
    for i in range(2):
        for lane, target in ((0, beside), (1, above), (2, partner)):
            copy = send(i, lane, sources[i], me, target)
            copy.start()
            sent.append(copy)
        place = pltpu.make_async_copy(sources[i], outs[i].at[me], place_sem.at[i])
        place.start()
        places.append(place)
    w_copies = []
    for c in range(PASSES):
        columns = pl.ds(c * width, width)
        w_copies.append(
            pltpu.make_async_copy(w_hbm.at[:, columns], w_ref.at[:, columns], w_sem.at[c])
        )
        w_copies[c].start()

    own = find(owner_ref, me)
    length = length_ref[0]
    groups = kv_width // HEAD_DIM
    per_group = UNITS // groups

    top_ref[...] = jnp.full_like(top_ref, FAR)
    acc_ref[...] = jnp.zeros_like(acc_ref)
    vt_ref[:, HEAD_DIM:, :] = jnp.ones((groups, 16, vt_ref.shape[2]), jnp.bfloat16)

    def stack(b, _):
        for h in range(UNITS * per_unit):
            block = q_ref[:, b, :, h * HEAD_DIM : (h + 1) * HEAD_DIM]
            at = h % per_unit * n * rows
            qs_ref[b * UNITS + h // per_unit, at : at + n * rows, :] = block.reshape(
                n * rows, HEAD_DIM
            )
        return 0

    lax.fori_loop(0, CHUNKS, stack, 0)

    def turn(s):
        place = pl.ds(pl.multiple_of(s * stretch, stretch), stretch)
        for g in range(groups):
            vt_ref[g, :HEAD_DIM, place] = all_v[s, :, g * HEAD_DIM : (g + 1) * HEAD_DIM].T

    lane = lax.broadcasted_iota(jnp.int32, (1, lanes), 1)
    lane = lane // rows % n * (CHUNKS * rows) + lane % rows
    scale = HEAD_DIM ** (-0.5) * LOG2E

    def score(b, u, s, c):
        g = u // per_group
        part = slice(c * piece, (c + 1) * piece)
        scores = lax.dot_general(
            all_k[s, part, g * HEAD_DIM : (g + 1) * HEAD_DIM], qs_ref[b * UNITS + u],
            (((1,), (1,)), ((), ())), preferred_element_type=jnp.float32,
        )
        score_ref[u, part, :] = scores
        return jnp.max(scores, axis=0, keepdims=True)

    def score_all(b, u, s):
        high_ref[u] = functools.reduce(jnp.maximum, [score(b, u, s, c) for c in range(2)])

    def spread(b, u, s, hide, masked, ahead):
        slot = b * UNITS + u
        top = top_ref[slot]
        if masked:
            def seen(c):
                key = c * piece + lax.broadcasted_iota(jnp.int32, (piece, lanes), 0)
                part = score_ref[u, c * piece : (c + 1) * piece, :]
                return jnp.where(key <= lane + b * rows, part, FAR)

            high = functools.reduce(
                jnp.maximum, [jnp.max(seen(c), axis=0, keepdims=True) for c in range(2)]
            )
            new_top = jnp.maximum(top, high * scale)
            below = new_top
        else:
            def seen(c):
                return score_ref[u, c * piece : (c + 1) * piece, :]

            new_top = jnp.maximum(top, high_ref[u] * scale - hide)
            below = new_top + hide
        rescale = jnp.exp2(top - new_top)
        highest, weights = [], []
        acc = acc_ref[slot] * rescale
        for c in range(2):
            highest.append(score(*ahead, c))
            weights.append(jnp.exp2(seen(c) * scale - below).astype(jnp.bfloat16))
        place = pl.ds(pl.multiple_of(s * stretch, stretch), stretch)
        acc = acc + jnp.dot(
            vt_ref[u // per_group, :, place], jnp.concatenate(weights, axis=0),
            preferred_element_type=jnp.float32,
        )
        acc_ref[slot] = acc
        top_ref[slot] = new_top
        high_ref[ahead[1]] = functools.reduce(jnp.maximum, highest)

    def run(count, place, masked=False):
        score_all(*(lambda b, s: (b, 0, s))(*place(0)))

        def body(k, _):
            b, s = place(k)
            later = place(jnp.minimum(k + 1, count - 1))
            hide = jnp.where(find(owner_ref, s) < own, 0.0, -FAR).astype(jnp.float32)
            for u in range(UNITS):
                ahead = (b, u + 1, s) if u + 1 < UNITS else (later[0], 0, later[1])
                spread(b, u, s, hide, masked, ahead)
            return 0

        lax.fori_loop(0, count, body, 0)

    for place in places:
        place.wait()
    turn(me)
    run(CHUNKS, lambda k: (k, me), True)

    sent[2].wait_recv()
    sent[5].wait_recv()
    turn(partner)
    run(CHUNKS, lambda k: (k, partner))

    relays = []
    for i in range(2):
        sent[3 * i].wait_recv()
        sent[3 * i + 1].wait_recv()
        relay = send(i, 3, outs[i].at[relay_from], relay_from, relay_to)
        relay.start()
        relays.append(relay)
        for hop, owner in ((4, beside), (5, above)):
            copy = send(i, hop, outs[i].at[owner], owner, partner)
            copy.start()
            relays.append(copy)
    turn(beside)
    run(CHUNKS, lambda k: (k, beside))
    last = []
    for i in range(2):
        relays[3 * i].wait_recv()
        copy = send(i, 6, outs[i].at[across], across, partner)
        copy.start()
        last.append(copy)
    turn(above)
    turn(across)
    for i in range(2):
        relays[3 * i + 1].wait_recv()
        relays[3 * i + 2].wait_recv()
        last[i].wait_recv()
    turn(source(3))
    turn(source(5))
    turn(source(7))

    def hops(j):
        toward = 1 - 2 * (j % 2)
        return (z + toward + n) % n, (z - toward + n) % n

    def carry(kind, j, target):
        origin, dest = ((out_far, in_far), (out_near, in_near), (out_sum, in_sum))[kind]
        return pltpu.make_async_remote_copy(
            src_ref=origin.at[j],
            dst_ref=dest.at[j],
            send_sem=sum_send.at[kind, j],
            recv_sem=sum_recv.at[kind, j],
            device_id={"tp": target},
            device_id_type=MESH,
        )

    def relay_sum(j, _):
        toward, away = hops(j)
        carry(0, j, toward).wait_recv()
        out_sum[j] = (mid_ref[j] + in_far[j].astype(jnp.float32)).astype(jnp.bfloat16)
        carry(2, j, toward).start()
        return 0

    def rows_of(device):
        return pl.ds(pl.multiple_of(device * rows, rows), rows)

    caches = [
        pltpu.make_async_copy(stage.at[i], out, cache_sem.at[i])
        for i, out in enumerate((kc_ref, vc_ref))
    ]

    def project(j, _):
        toward, away = hops(j)
        for t in range(width // SLICE):
            start = pl.multiple_of(j % PASSES * width + t * SLICE, SLICE)
            to = slice(t * SLICE, (t + 1) * SLICE)
            score_ref[0, : n * rows, :] = jnp.dot(
                att_ref[...], w_ref[:, pl.ds(start, SLICE)], preferred_element_type=jnp.float32
            )
            out_far[j, :, to] = score_ref[0, rows_of((z + 2) % n), :].astype(jnp.bfloat16)
            out_near[j, :, to] = score_ref[0, rows_of(away), :].astype(jnp.bfloat16)
            mid_ref[j, :, to] = score_ref[0, rows_of(toward), :]
            own_ref[j, :, to] = score_ref[0, rows_of(z), :]
        carry(0, j, toward).start()
        carry(1, j, away).start()
        return 0

    def chunk(b, _):
        run(5, lambda k: (b, source(k + 3)))

        @pl.when(b > 0)
        def _():
            lax.fori_loop((b - 1) * PASSES, b * PASSES, relay_sum, 0)

        alive = (own * stretch + lane + b * rows < length).astype(jnp.float32)
        for u in range(UNITS):
            slot = b * UNITS + u
            total = acc_ref[slot, HEAD_DIM : HEAD_DIM + 1]
            out = (acc_ref[slot, :HEAD_DIM] * (alive / total)).T.astype(jnp.bfloat16)
            for h in range(per_unit):
                column = (u * per_unit + h) * HEAD_DIM
                att_ref[:, column : column + HEAD_DIM] = out[h * n * rows : (h + 1) * n * rows]

        @pl.when(b == 0)
        def _():
            for copy in w_copies:
                copy.wait()

        lax.fori_loop(b * PASSES, (b + 1) * PASSES, project, 0)

        @pl.when(b == 0)
        def _():
            kept = jnp.where(home_ref[0] == me, length_ref[0], 0)

            def fill(j, _):
                target = pl.ds(pl.multiple_of(j * stretch, stretch), stretch)
                position = j * stretch + lax.broadcasted_iota(jnp.int32, (stretch, kv_width), 0)
                for i, gathered in enumerate(outs):
                    block = gathered[owner_ref[j]]
                    stage[i, target, :] = jnp.where(position < kept, block, jnp.zeros_like(block))
                return 0

            lax.fori_loop(0, MAX_STRETCHES, fill, 0)
            for copy in caches:
                copy.start()

        return 0

    lax.fori_loop(0, CHUNKS, chunk, 0)
    lax.fori_loop(steps - PASSES, steps, relay_sum, 0)

    for j in range(steps):
        toward, away = hops(j)
        carry(1, j, away).wait_recv()
        carry(2, j, toward).wait_recv()
        total = own_ref[j] + in_near[j].astype(jnp.float32) + in_sum[j].astype(jnp.float32)
        b, c = j // PASSES, j % PASSES
        o_ref[b * rows : (b + 1) * rows, c * width : (c + 1) * width] = total.astype(jnp.bfloat16)
    for j in range(steps):
        toward, away = hops(j)
        carry(0, j, toward).wait_send()
        carry(1, j, away).wait_send()
        carry(2, j, toward).wait_send()
    for copy in sent + relays + last:
        copy.wait_send()
    for copy in caches:
        copy.wait()


def layer(tables, queries, keys, values, w_out):
    stretch, depth = queries.shape
    kv_width = keys.shape[1]
    groups = kv_width // HEAD_DIM
    features = w_out.shape[1]
    replicas, n = lax.axis_size("sp"), lax.axis_size("tp")
    rows = stretch // (n * CHUNKS)
    steps = CHUNKS * PASSES
    lanes = depth // HEAD_DIM // UNITS * n * rows
    span = replicas * stretch
    slots = CHUNKS * UNITS
    cache = jax.ShapeDtypeStruct((span, kv_width), jnp.bfloat16)
    gathered = pltpu.VMEM((replicas, stretch, kv_width), jnp.bfloat16)
    held = pltpu.VMEM((steps, rows, features // PASSES), jnp.float32)
    moved = pltpu.VMEM((steps, rows, features // PASSES), jnp.bfloat16)
    whole = pl.BlockSpec(memory_space=pltpu.VMEM)
    scalar = pl.BlockSpec(memory_space=pltpu.SMEM)
    anywhere = pl.BlockSpec(memory_space=pl.ANY)
    return pl.pallas_call(
        layer_kernel,
        out_shape=[jax.ShapeDtypeStruct((stretch // n, features), jnp.bfloat16), cache, cache],
        in_specs=[scalar] * 3 + [whole] * 3 + [anywhere],
        out_specs=[whole, anywhere, anywhere],
        scratch_shapes=[
            gathered,
            gathered,
            pltpu.VMEM((depth, features), jnp.bfloat16),
            pltpu.VMEM((groups, HEAD_DIM + 16, span), jnp.bfloat16),
            pltpu.VMEM((slots, lanes, HEAD_DIM), jnp.bfloat16),
            pltpu.VMEM((slots, 1, lanes), jnp.float32),
            pltpu.VMEM((slots, HEAD_DIM + 16, lanes), jnp.float32),
            pltpu.VMEM((UNITS, 1, lanes), jnp.float32),
            pltpu.VMEM((UNITS, stretch, lanes), jnp.float32),
            pltpu.VMEM((n * rows, depth), jnp.bfloat16),
            pltpu.VMEM((2, span, kv_width), jnp.bfloat16),
            held, held, moved, moved, moved, moved, moved, moved,
            pltpu.SemaphoreType.DMA((PASSES,)),
            pltpu.SemaphoreType.DMA((2,)),
            pltpu.SemaphoreType.DMA((2,)),
            pltpu.SemaphoreType.DMA((7, 2)),
            pltpu.SemaphoreType.DMA((7, 2)),
            pltpu.SemaphoreType.DMA((3, steps)),
            pltpu.SemaphoreType.DMA((3, steps)),
        ],
        compiler_params=pltpu.CompilerParams(
            collective_id=0, has_side_effects=True, vmem_limit_bytes=60 * 2**20
        ),
        name="layer",
    )(*tables, queries.reshape(n, CHUNKS, rows, depth), keys, values, w_out)


def shards(queries, keys, values, w_out, lengths, stretch_owner, home_replica):
    stretch = queries.shape[0]
    tables = (stretch_owner, lengths, home_replica)
    if lax.axis_size("sp") == 8 and lax.axis_size("tp") == 4 and lengths.shape[0] == 1:
        return layer(tables, queries, keys, values, w_out)
    all_keys, all_values = gather(keys, values)
    attended, kept_keys, kept_values = attend(stretch, tables, queries, all_keys, all_values)
    return (project(attended, w_out), kept_keys, kept_values)


def solution(mesh):
    placed = (P("sp", "tp"), P("sp", "tp"), P("sp", "tp"), P("tp", None), P(), P(), P())
    return jax.shard_map(
        shards,
        mesh=mesh,
        in_specs=placed,
        out_specs=(P(("sp", "tp"), None), P("sp", "tp"), P("sp", "tp")),
        check_vma=False,
    )
```

profile of v0, /device:TPU:0, one launch (start us, length us, event | category | flops | bytes accessed | tf_op | source)
XLA Modules:
  0.0 118.8 jit_solution(16417574273588287615)
XLA Ops:
  1.9 110.7 %layer.1 = (bf16[128,4096]{1,0:T(8,128)(2,1)}, bf16[4096,256]{1,0:T(8,128)(2,1)}, bf16[4096,256]{1,0:T(8,128)(2,1)}) custom-call(s32[8]{0:T(128)} %owner_ref.1, s32[1]{0:T(128)S(6)} %copy.13.length_ref, s32[1]{0:T(128)S(6)} %copy.14.home_ref, bf16[4,4,32,2048]{3,2,1,0:T(8,128)(2,1)} %bitcast.1, bf16[512,256]{1,0:T(8,128)(2,1)} %k_ref.1, ...), custom_call_target="tpu_custom_call" | custom-call | tf_op jit(solution)/shard_map/layer/pallas_call | solution.py:538
  112.7 0.0 copy-start.1
  112.7 2.4 %copy.15 = bf16[128,4096]{1,0:T(8,128)(2,1)} copy(bf16[128,4096]{1,0:T(8,128)(2,1)} %get-tuple-element.6) | data formatting | bytes 2097152
  115.1 0.0 copy-done.1
  115.1 0.0 copy-start
  115.1 1.3 %copy.16 = bf16[4096,256]{1,0:T(8,128)(2,1)} copy(bf16[4096,256]{1,0:T(8,128)(2,1)S(1)} %copy-done.1) | data formatting | bytes 4194304
  116.4 1.0 copy-done
  117.5 1.3 %copy.17 = bf16[4096,256]{1,0:T(8,128)(2,1)} copy(bf16[4096,256]{1,0:T(8,128)(2,1)S(1)} %copy-done) | data formatting | bytes 4194304
Async XLA Ops:
  112.7 2.4 %copy-start.1 = (bf16[4096,256]{1,0:T(8,128)(2,1)S(1)}, bf16[4096,256]{1,0:T(8,128)(2,1)}, u32[]{:S(2)}) copy-start(bf16[4096,256]{1,0:T(8,128)(2,1)} %get-tuple-element.7) | copy-start | bytes 6291460
  115.1 2.3 %copy-start = (bf16[4096,256]{1,0:T(8,128)(2,1)S(1)}, bf16[4096,256]{1,0:T(8,128)(2,1)}, u32[]{:S(2)}) copy-start(bf16[4096,256]{1,0:T(8,128)(2,1)} %get-tuple-element.8) | copy-start | bytes 6291460
where the time goes:
time: 119 us
  Pallas kernels  111 us (93%)
  local copies, waits for them, and re-layouts  6.11 us (5%)
  between operations  1.94 us (2%)
    pallas_call x1, Pallas kernels, layer(): pl.pallas_call(layer_kernel, out_shape=[jax.ShapeDtypeStruct((stretch //...  111 us
    unnamed x7, local copies, waits for them, and re-layouts  6.11 us

commit v1 on v0

--- a/solution.py
+++ b/solution.py
@@ -212,19 +212,19 @@
 UNITS = 4
 PASSES = 2
 SLICE = 512
+VMEM_LIMIT = 54
 
 
 def layer_kernel(
-    owner_ref, length_ref, home_ref, q_ref, k_ref, v_ref, w_hbm, o_ref, kc_ref, vc_ref,
-    all_k, all_v, w_ref, vt_ref, qs_ref, top_ref, acc_ref, high_ref, score_ref, att_ref, stage,
-    own_ref, mid_ref, out_far, out_near, out_sum, in_far, in_near, in_sum,
-    w_sem, place_sem, cache_sem, send_sem, recv_sem, sum_send, sum_recv,
+    owner_ref, length_ref, home_ref, q_hbm, k_hbm, v_hbm, w_hbm, o_ref, kc_ref, vc_ref,
+    all_k, all_v, q_ref, w_ref, vt_ref, top_ref, acc_ref, high_ref, score_ref, att_ref, stage,
+    part_ref, right_ref, left_ref,
+    q_sem, w_sem, place_sem, cache_sem, send_sem, recv_sem, sum_send, sum_recv,
 ):
     me = lax.axis_index("sp")
     z = lax.axis_index("tp")
     n = 4
-    stretch = k_ref.shape[0]
-    kv_width = k_ref.shape[1]
+    stretch, kv_width = all_k.shape[1:]
     rows = q_ref.shape[2]
     lanes = score_ref.shape[2]
     per_unit = lanes // (n * rows)
@@ -246,11 +246,25 @@
     barrier = pltpu.get_barrier_semaphore()
     for other in (beside, above, partner):
         pl.semaphore_signal(barrier, inc=1, device_id={"sp": other}, device_id_type=MESH)
-    for other in ((z + 1) % n, (z + n - 1) % n):
-        pl.semaphore_signal(barrier, inc=1, device_id={"tp": other}, device_id_type=MESH)
-    pl.semaphore_wait(barrier, 5)
-
-    sources, outs = (k_ref, v_ref), (all_k, all_v)
+
+    @pl.when(z > 0)
+    def _():
+        pl.semaphore_signal(barrier, inc=1, device_id={"tp": z - 1}, device_id_type=MESH)
+
+    @pl.when(z < n - 1)
+    def _():
+        pl.semaphore_signal(barrier, inc=1, device_id={"tp": z + 1}, device_id_type=MESH)
+
+    sources, outs = (k_hbm, v_hbm), (all_k, all_v)
+    places = [
+        pltpu.make_async_copy(sources[i], outs[i].at[me], place_sem.at[i]) for i in range(2)
+    ]
+    for place in places:
+        place.start()
+    q_copy = pltpu.make_async_copy(q_hbm, q_ref, q_sem)
+    q_copy.start()
+
+    pl.semaphore_wait(barrier, 3 + jnp.minimum(z, 1) + jnp.minimum(n - 1 - z, 1))
 
     def send(i, lane, source, owner, target):
         return pltpu.make_async_remote_copy(
@@ -262,15 +276,12 @@
             device_id_type=MESH,
         )
 
-    sent, places = [], []
+    sent = []
     for i in range(2):
         for lane, target in ((0, beside), (1, above), (2, partner)):
             copy = send(i, lane, sources[i], me, target)
             copy.start()
             sent.append(copy)
-        place = pltpu.make_async_copy(sources[i], outs[i].at[me], place_sem.at[i])
-        place.start()
-        places.append(place)
     w_copies = []
     for c in range(PASSES):
         columns = pl.ds(c * width, width)
@@ -288,17 +299,6 @@
     acc_ref[...] = jnp.zeros_like(acc_ref)
     vt_ref[:, HEAD_DIM:, :] = jnp.ones((groups, 16, vt_ref.shape[2]), jnp.bfloat16)
 
-    def stack(b, _):
-        for h in range(UNITS * per_unit):
-            block = q_ref[:, b, :, h * HEAD_DIM : (h + 1) * HEAD_DIM]
-            at = h % per_unit * n * rows
-            qs_ref[b * UNITS + h // per_unit, at : at + n * rows, :] = block.reshape(
-                n * rows, HEAD_DIM
-            )
-        return 0
-
-    lax.fori_loop(0, CHUNKS, stack, 0)
-
     def turn(s):
         place = pl.ds(pl.multiple_of(s * stretch, stretch), stretch)
         for g in range(groups):
@@ -311,8 +311,12 @@
     def score(b, u, s, c):
         g = u // per_group
         part = slice(c * piece, (c + 1) * piece)
+        query = [
+            q_ref[:, b, :, h * HEAD_DIM : (h + 1) * HEAD_DIM].reshape(n * rows, HEAD_DIM)
+            for h in range(u * per_unit, (u + 1) * per_unit)
+        ]
         scores = lax.dot_general(
-            all_k[s, part, g * HEAD_DIM : (g + 1) * HEAD_DIM], qs_ref[b * UNITS + u],
+            all_k[s, part, g * HEAD_DIM : (g + 1) * HEAD_DIM], jnp.concatenate(query, axis=0),
             (((1,), (1,)), ((), ())), preferred_element_type=jnp.float32,
         )
         score_ref[u, part, :] = scores
@@ -356,8 +360,8 @@
         top_ref[slot] = new_top
         high_ref[ahead[1]] = functools.reduce(jnp.maximum, highest)
 
-    def run(count, place, masked=False):
-        score_all(*(lambda b, s: (b, 0, s))(*place(0)))
+    def run(first, count, place, masked=False):
+        score_all(*(lambda b, s: (b, 0, s))(*place(first)))
 
         def body(k, _):
             b, s = place(k)
@@ -368,20 +372,22 @@
                 spread(b, u, s, hide, masked, ahead)
             return 0
 
-        lax.fori_loop(0, count, body, 0)
+        lax.fori_loop(first, count, body, 0)
 
     for place in places:
         place.wait()
     turn(me)
-    run(CHUNKS, lambda k: (k, me), True)
-
-    sent[2].wait_recv()
-    sent[5].wait_recv()
+    q_copy.wait()
+    run(0, CHUNKS, lambda k: (k, me), True)
+
+    for i in range(2):
+        sent[3 * i + 2].wait_recv()
     turn(partner)
-    run(CHUNKS, lambda k: (k, partner))
-
-    relays = []
-    for i in range(2):
+    run(0, 2, lambda k: (k, partner))
+
+    relays, last = [], []
+
+    def pass_on(i):
         sent[3 * i].wait_recv()
         sent[3 * i + 1].wait_recv()
         relay = send(i, 3, outs[i].at[relay_from], relay_from, relay_to)
@@ -391,48 +397,81 @@
             copy = send(i, hop, outs[i].at[owner], owner, partner)
             copy.start()
             relays.append(copy)
-    turn(beside)
-    run(CHUNKS, lambda k: (k, beside))
-    last = []
-    for i in range(2):
+
+    def share(i):
         relays[3 * i].wait_recv()
         copy = send(i, 6, outs[i].at[across], across, partner)
         copy.start()
         last.append(copy)
+
+    pass_on(0)
+    run(2, CHUNKS, lambda k: (k, partner))
+    pass_on(1)
+    turn(beside)
     turn(above)
-    turn(across)
+    run(1, 3, lambda k: (0, source(2 * k)))
+    share(0)
     for i in range(2):
         relays[3 * i + 1].wait_recv()
         relays[3 * i + 2].wait_recv()
-        last[i].wait_recv()
     turn(source(3))
     turn(source(5))
+    run(1, 3, lambda k: (0, source(2 * k + 1)))
+    share(1)
+    turn(across)
+    run(0, 1, lambda k: (0, across))
+    for i in range(2):
+        last[i].wait_recv()
     turn(source(7))
 
-    def hops(j):
-        toward = 1 - 2 * (j % 2)
-        return (z + toward + n) % n, (z - toward + n) % n
-
-    def carry(kind, j, target):
-        origin, dest = ((out_far, in_far), (out_near, in_near), (out_sum, in_sum))[kind]
+    def wire(way, j, d):
         return pltpu.make_async_remote_copy(
-            src_ref=origin.at[j],
-            dst_ref=dest.at[j],
-            send_sem=sum_send.at[kind, j],
-            recv_sem=sum_recv.at[kind, j],
-            device_id={"tp": target},
+            src_ref=part_ref.at[j, d],
+            dst_ref=(right_ref, left_ref)[way].at[j, d],
+            send_sem=sum_send.at[j, d],
+            recv_sem=sum_recv.at[way, j, d],
+            device_id={"tp": (z + 1 - 2 * way + n) % n},
             device_id_type=MESH,
         )
 
+    flows = (
+        ((0, 0, (3, 2, 1)), (n - 1, 1, (0, 1, 2))),
+        ((1, 0, (3, 2)), (n - 2, 1, (0, 1))),
+        ((2, 0, (3,)), (n - 3, 1, (0,))),
+    )
+
+    def each(hop, step):
+        for at, way, order in flows[hop]:
+            @pl.when(z == at)
+            def _(way=way, order=order):
+                for d in order:
+                    step(way, d)
+
+    def begin(js):
+        def step(way, d):
+            for j in js:
+                wire(way, j, d).start()
+
+        each(0, step)
+
+    def relay(hop, j):
+        def step(way, d):
+            wire(way, j, d).wait_recv()
+            came = (right_ref, left_ref)[way][j, d].astype(jnp.float32)
+            total = part_ref[j, d].astype(jnp.float32) + came
+            part_ref[j, d] = total.astype(jnp.bfloat16)
+            wire(way, j, d).start()
+
+        each(hop, step)
+
     def relay_sum(j, _):
-        toward, away = hops(j)
-        carry(0, j, toward).wait_recv()
-        out_sum[j] = (mid_ref[j] + in_far[j].astype(jnp.float32)).astype(jnp.bfloat16)
-        carry(2, j, toward).start()
+        relay(1, j)
+
+        @pl.when(j > 0)
+        def _():
+            relay(2, j - 1)
+
         return 0
-
-    def rows_of(device):
-        return pl.ds(pl.multiple_of(device * rows, rows), rows)
 
     caches = [
         pltpu.make_async_copy(stage.at[i], out, cache_sem.at[i])
@@ -440,23 +479,23 @@
     ]
 
     def project(j, _):
-        toward, away = hops(j)
         for t in range(width // SLICE):
             start = pl.multiple_of(j % PASSES * width + t * SLICE, SLICE)
-            to = slice(t * SLICE, (t + 1) * SLICE)
-            score_ref[0, : n * rows, :] = jnp.dot(
+            partial = jnp.dot(
                 att_ref[...], w_ref[:, pl.ds(start, SLICE)], preferred_element_type=jnp.float32
             )
-            out_far[j, :, to] = score_ref[0, rows_of((z + 2) % n), :].astype(jnp.bfloat16)
-            out_near[j, :, to] = score_ref[0, rows_of(away), :].astype(jnp.bfloat16)
-            mid_ref[j, :, to] = score_ref[0, rows_of(toward), :]
-            own_ref[j, :, to] = score_ref[0, rows_of(z), :]
-        carry(0, j, toward).start()
-        carry(1, j, away).start()
+            part_ref[j, :, :, t * SLICE : (t + 1) * SLICE] = partial.astype(jnp.bfloat16).reshape(
+                n, rows, SLICE
+            )
+
+        @pl.when(j < PASSES)
+        def _():
+            begin([j])
+
         return 0
 
     def chunk(b, _):
-        run(5, lambda k: (b, source(k + 3)))
+        run(jnp.where(b == 0, 7, 2), 8, lambda k: (b, source(k)))
 
         @pl.when(b > 0)
         def _():
@@ -478,43 +517,105 @@
 
         lax.fori_loop(b * PASSES, (b + 1) * PASSES, project, 0)
 
-        @pl.when(b == 0)
+        @pl.when(b > 0)
         def _():
-            kept = jnp.where(home_ref[0] == me, length_ref[0], 0)
-
-            def fill(j, _):
-                target = pl.ds(pl.multiple_of(j * stretch, stretch), stretch)
-                position = j * stretch + lax.broadcasted_iota(jnp.int32, (stretch, kv_width), 0)
-                for i, gathered in enumerate(outs):
-                    block = gathered[owner_ref[j]]
-                    stage[i, target, :] = jnp.where(position < kept, block, jnp.zeros_like(block))
-                return 0
-
-            lax.fori_loop(0, MAX_STRETCHES, fill, 0)
-            for copy in caches:
-                copy.start()
+            begin([b * PASSES + c for c in range(PASSES)])
 
         return 0
 
     lax.fori_loop(0, CHUNKS, chunk, 0)
+
+    kept = jnp.where(home_ref[0] == me, length, 0)
+
+    def fill(j, _):
+        target = pl.ds(pl.multiple_of(j * stretch, stretch), stretch)
+        position = j * stretch + lax.broadcasted_iota(jnp.int32, (stretch, kv_width), 0)
+        for i, gathered in enumerate(outs):
+            block = gathered[owner_ref[j]]
+            stage[i, target, :] = jnp.where(position < kept, block, jnp.zeros_like(block))
+        return 0
+
+    lax.fori_loop(0, MAX_STRETCHES, fill, 0)
+    for copy in caches:
+        copy.start()
     lax.fori_loop(steps - PASSES, steps, relay_sum, 0)
+    relay(2, steps - 1)
 
     for j in range(steps):
-        toward, away = hops(j)
-        carry(1, j, away).wait_recv()
-        carry(2, j, toward).wait_recv()
-        total = own_ref[j] + in_near[j].astype(jnp.float32) + in_sum[j].astype(jnp.float32)
         b, c = j // PASSES, j % PASSES
-        o_ref[b * rows : (b + 1) * rows, c * width : (c + 1) * width] = total.astype(jnp.bfloat16)
+        out = o_ref.at[b * rows : (b + 1) * rows, c * width : (c + 1) * width]
+        total = part_ref[j, z].astype(jnp.float32)
+
+        @pl.when(z > 0)
+        def _(j=j):
+            wire(0, j, z).wait_recv()
+
+        @pl.when(z < n - 1)
+        def _(j=j):
+            wire(1, j, z).wait_recv()
+
+        @pl.when(z == 0)
+        def _(j=j, out=out, total=total):
+            out[...] = (total + left_ref[j, z].astype(jnp.float32)).astype(jnp.bfloat16)
+
+        @pl.when(z == n - 1)
+        def _(j=j, out=out, total=total):
+            out[...] = (total + right_ref[j, z].astype(jnp.float32)).astype(jnp.bfloat16)
+
+        @pl.when((z > 0) & (z < n - 1))
+        def _(j=j, out=out, total=total):
+            came = right_ref[j, z].astype(jnp.float32) + left_ref[j, z].astype(jnp.float32)
+            out[...] = (total + came).astype(jnp.bfloat16)
+
     for j in range(steps):
-        toward, away = hops(j)
-        carry(0, j, toward).wait_send()
-        carry(1, j, away).wait_send()
-        carry(2, j, toward).wait_send()
+        for hop in range(n - 1):
+            each(hop, lambda way, d, j=j: wire(way, j, d).wait_send())
     for copy in sent + relays + last:
         copy.wait_send()
     for copy in caches:
         copy.wait()
+
+
+def finish_kernel(mixed, keys, values, o_ref, kc_ref, vc_ref, hold, kept, in_sem, out_sem):
+    half = kept.shape[2]
+    moves = [(mixed, hold, o_ref)]
+    for i, (source, out) in enumerate(((keys, kc_ref), (values, vc_ref))):
+        for c in range(2):
+            rows = pl.ds(c * half, half)
+            moves.append((source.at[rows], kept.at[i, c], out.at[rows]))
+    coming = [
+        pltpu.make_async_copy(source, middle, in_sem.at[k])
+        for k, (source, middle, _) in enumerate(moves)
+    ]
+    going = [
+        pltpu.make_async_copy(middle, out, out_sem.at[k])
+        for k, (_, middle, out) in enumerate(moves)
+    ]
+    for copy in coming:
+        copy.start()
+    for before, after in zip(coming, going):
+        before.wait()
+        after.start()
+    for copy in going:
+        copy.wait()
+
+
+def finish(results):
+    mixed, keys, _ = results
+    anywhere = pl.BlockSpec(memory_space=pl.ANY)
+    return pl.pallas_call(
+        finish_kernel,
+        out_shape=[jax.ShapeDtypeStruct(r.shape, r.dtype) for r in results],
+        in_specs=[anywhere] * 3,
+        out_specs=[anywhere] * 3,
+        scratch_shapes=[
+            pltpu.VMEM(mixed.shape, mixed.dtype),
+            pltpu.VMEM((2, 2, keys.shape[0] // 2, keys.shape[1]), keys.dtype),
+            pltpu.SemaphoreType.DMA((5,)),
+            pltpu.SemaphoreType.DMA((5,)),
+        ],
+        name="finish",
+    )(*results)
 
 
 def layer(tables, queries, keys, values, w_out):
@@ -530,39 +631,39 @@
     slots = CHUNKS * UNITS
     cache = jax.ShapeDtypeStruct((span, kv_width), jnp.bfloat16)
     gathered = pltpu.VMEM((replicas, stretch, kv_width), jnp.bfloat16)
-    held = pltpu.VMEM((steps, rows, features // PASSES), jnp.float32)
-    moved = pltpu.VMEM((steps, rows, features // PASSES), jnp.bfloat16)
+    moved = pltpu.VMEM((steps, n, rows, features // PASSES), jnp.bfloat16)
     whole = pl.BlockSpec(memory_space=pltpu.VMEM)
     scalar = pl.BlockSpec(memory_space=pltpu.SMEM)
     anywhere = pl.BlockSpec(memory_space=pl.ANY)
     return pl.pallas_call(
         layer_kernel,
         out_shape=[jax.ShapeDtypeStruct((stretch // n, features), jnp.bfloat16), cache, cache],
-        in_specs=[scalar] * 3 + [whole] * 3 + [anywhere],
+        in_specs=[scalar] * 3 + [anywhere] * 4,
         out_specs=[whole, anywhere, anywhere],
         scratch_shapes=[
             gathered,
             gathered,
+            pltpu.VMEM((n, CHUNKS, rows, depth), jnp.bfloat16),
             pltpu.VMEM((depth, features), jnp.bfloat16),
             pltpu.VMEM((groups, HEAD_DIM + 16, span), jnp.bfloat16),
-            pltpu.VMEM((slots, lanes, HEAD_DIM), jnp.bfloat16),
             pltpu.VMEM((slots, 1, lanes), jnp.float32),
             pltpu.VMEM((slots, HEAD_DIM + 16, lanes), jnp.float32),
             pltpu.VMEM((UNITS, 1, lanes), jnp.float32),
             pltpu.VMEM((UNITS, stretch, lanes), jnp.float32),
             pltpu.VMEM((n * rows, depth), jnp.bfloat16),
             pltpu.VMEM((2, span, kv_width), jnp.bfloat16),
-            held, held, moved, moved, moved, moved, moved, moved,
+            moved, moved, moved,
+            pltpu.SemaphoreType.DMA,
             pltpu.SemaphoreType.DMA((PASSES,)),
             pltpu.SemaphoreType.DMA((2,)),
             pltpu.SemaphoreType.DMA((2,)),
             pltpu.SemaphoreType.DMA((7, 2)),
             pltpu.SemaphoreType.DMA((7, 2)),
-            pltpu.SemaphoreType.DMA((3, steps)),
-            pltpu.SemaphoreType.DMA((3, steps)),
+            pltpu.SemaphoreType.DMA((steps, n)),
+            pltpu.SemaphoreType.DMA((2, steps, n)),
         ],
         compiler_params=pltpu.CompilerParams(
-            collective_id=0, has_side_effects=True, vmem_limit_bytes=60 * 2**20
+            collective_id=0, has_side_effects=True, vmem_limit_bytes=VMEM_LIMIT * 2**20
         ),
         name="layer",
     )(*tables, queries.reshape(n, CHUNKS, rows, depth), keys, values, w_out)
@@ -572,7 +673,7 @@
     stretch = queries.shape[0]
     tables = (stretch_owner, lengths, home_replica)
     if lax.axis_size("sp") == 8 and lax.axis_size("tp") == 4 and lengths.shape[0] == 1:
-        return layer(tables, queries, keys, values, w_out)
+        return tuple(finish(layer(tables, queries, keys, values, w_out)))
     all_keys, all_values = gather(keys, values)
     attended, kept_keys, kept_values = attend(stretch, tables, queries, all_keys, all_values)
     return (project(attended, w_out), kept_keys, kept_values)

time: 119 us -> 112 us (0.941)
  local copies, waits for them, and re-layouts: 6.11 us -> 0 us
    unnamed x7 -> x0, local copies, waits for them, and re-layouts: 6.11 us -> none
    pallas_call x1, Pallas kernels: 111 us -> 106 us  [layer(): pl.pallas_call(layer_kernel, out_shape=[jax.ShapeDtypeStruct((stretch //...]
    pallas_call x0 -> x1, Pallas kernels: none -> 4.38 us  [finish(): pl.pallas_call(finish_kernel, out_shape=[jax.ShapeDtypeStruct(r.shape, r....]
where the time goes in v1:
time: 112 us
  Pallas kernels  110 us (98%)
  between operations  2.09 us (2%)
    pallas_call x1, Pallas kernels, layer(): pl.pallas_call(layer_kernel, out_shape=[jax.ShapeDtypeStruct((stretch //...  106 us
    pallas_call x1, Pallas kernels, finish(): pl.pallas_call(finish_kernel, out_shape=[jax.ShapeDtypeStruct(r.shape, r....  4.38 us

profile of v1, /device:TPU:0, one launch (start us, length us, event | category | flops | bytes accessed | tf_op | source)
XLA Modules:
  0.0 112.3 jit_solution(3506441337827893683)
XLA Ops:
  1.9 105.8 %layer.1 = (bf16[128,4096]{1,0:T(8,128)(2,1)}, bf16[4096,256]{1,0:T(8,128)(2,1)}, bf16[4096,256]{1,0:T(8,128)(2,1)}) custom-call(s32[8]{0:T(128)} %owner_ref.1, s32[1]{0:T(128)S(6)} %copy.10.length_ref, s32[1]{0:T(128)S(6)} %copy.11.home_ref, bf16[4,4,32,2048]{3,2,1,0:T(8,128)(2,1)} %bitcast.1, bf16[512,256]{1,0:T(8,128)(2,1)} %k_hbm.1, ...), custom_call_target="tpu_custom_call" | custom-call | tf_op jit(solution)/shard_map/layer/pallas_call | solution.py:638
  107.7 4.4 %finish.1 = (bf16[128,4096]{1,0:T(8,128)(2,1)}, bf16[4096,256]{1,0:T(8,128)(2,1)}, bf16[4096,256]{1,0:T(8,128)(2,1)}) custom-call(bf16[128,4096]{1,0:T(8,128)(2,1)} %get-tuple-element.6.mixed, bf16[4096,256]{1,0:T(8,128)(2,1)} %get-tuple-element.7.keys, bf16[4096,256]{1,0:T(8,128)(2,1)} %get-tuple-element.8.values), custom_call_target="tpu_custom_call" | custom-call | tf_op jit(solution)/shard_map/finish/pallas_call | solution.py:606
